TPU v7x, 32 devices: a whole 2x2x4 slice. The times are simulated.
32 devices in a mesh: layer: 4 (over y, x), expert: 4 (over z), dp: 2 (over core).
Axes of the slice: x: 2, y: 2, z: 4, core: 2. Of those that a mesh axis runs over, the one named last changes fastest.
Arguments:
- tokens: bfloat16 [2048, 2304], P(('expert', 'dp')), may hold values from -6 to 6
- expert_ids: int32 [2048], P(('expert', 'dp')), may hold values from 0 to 3, as said below
- slot_ids: int32 [2048], P(('expert', 'dp')), may hold values from 0 to 127, as said below
- live_mask: int32 [2048], P(('expert', 'dp')), may hold values from 0 to 1
- w_enc: bfloat16 [4, 2304, 2048], P('expert', None, 'layer'), may hold values from -0.125 to 0.125
- b_enc: float32 [4, 2048], P('expert', 'layer'), may hold values from -3 to 3
- w_dec: bfloat16 [2, 4, 2048, 2304], P(None, 'expert', 'layer'), may hold values from -0.125 to 0.125
- b_dec: float32 [2, 2304], P(None, 'layer'), may hold values from -3 to 3
- targets: bfloat16 [2, 2048, 2304], P(None, ('expert', 'dp'), 'layer'), may hold values from -6 to 6
Outputs:
- recon: bfloat16 [2, 2048, 2304], P(None, ('expert', 'dp'), 'layer')
- grad_w_enc: bfloat16 [4, 2304, 2048], P('expert', 'dp', 'layer')
- grad_b_enc: float32 [4, 2048], P('expert', ('layer', 'dp'))
- grad_w_dec: bfloat16 [2, 4, 2048, 2304], P(None, 'expert', 'layer', 'dp')
- grad_b_dec: float32 [2, 2304], P(None, 'layer')
Inputs may be any that keep to these rules, and one draw needn't show every extreme that they name: `expert_ids`: the 256 tokens of one block name any expert at most 128 times; in every draw one expert is named exactly 128 times by every block. `slot_ids`: tokens of one block that name the same expert have distinct slots.
All inputs are finite; a program needn't handle non-finite values.
Results may differ from a plain program's by a relative error of at most 0.01.
Values may be sent and summed in bfloat16 or wider, within the bound.
A program may use at most 128 MiB of HBM per device.

v0:
```python
import math
import jax
import jax.numpy as jnp
from jax import lax
from jax.sharding import PartitionSpec as P


def place_rows(values, cell_index, total_cells):
    shape = values.shape[:-2] + (total_cells, values.shape[-1])
    zero_fill = jnp.zeros(shape, values.dtype)
    return zero_fill.at[..., cell_index, :].set(values)


def local(tokens, expert_ids, slot_ids, live_mask, w_enc, b_enc, w_dec, b_dec, targets):
    n_expert = lax.axis_size("expert")
    n_layer = lax.axis_size("layer")
    tok_rows, model_width = tokens.shape
    capacity = 2 * tok_rows // n_expert
    total_cells = n_expert * capacity
    cell_index = expert_ids * capacity + slot_ids
    quarter = model_width // n_layer
    targets_count = w_dec.shape[0]
    enc_weight = w_enc[0]
    dec_weight = w_dec[:, 0]
    outgoing = place_rows(tokens, cell_index, total_cells).reshape(n_expert, capacity, model_width)
    arrived = lax.all_to_all(outgoing, "expert", split_axis=0, concat_axis=0, tiled=True).reshape(
        total_cells, model_width
    )
    pre_act = jnp.dot(arrived, enc_weight, preferred_element_type=jnp.float32)
    pre_act = pre_act + b_enc[0][None, :]
    active = jnp.maximum(pre_act, 0.0)
    latents = (active * active).astype(jnp.bfloat16)
    partials = jnp.einsum(
        "rl,tld->trd", latents, dec_weight, preferred_element_type=jnp.float32
    ).astype(jnp.bfloat16)
    summed = lax.psum_scatter(
        lax.optimization_barrier(partials).astype(jnp.float32).astype(jnp.bfloat16),
        "layer",
        scatter_dimension=2,
        tiled=True,
    )
    outgoing_rec = summed.reshape(targets_count, n_expert, capacity, quarter)
    returned = lax.all_to_all(outgoing_rec, "expert", split_axis=1, concat_axis=1, tiled=True)
    recon_sum = returned.reshape(targets_count, total_cells, quarter)[:, cell_index, :]
    recon_full = lax.optimization_barrier(recon_sum).astype(jnp.float32) + b_dec[:, None, :]
    recon = recon_full.astype(jnp.bfloat16)
    coef = 2.0 / math.sqrt(tok_rows)
    live_wide = live_mask.astype(jnp.float32)
    error_grad = (
        coef * live_wide[None, :, None] * (recon_full - targets.astype(jnp.float32))
    ).astype(jnp.bfloat16)
    error_wide = lax.optimization_barrier(error_grad).astype(jnp.float32)
    grad_b_dec = lax.psum(jnp.sum(error_wide, axis=1), ("expert", "dp"))
    outgoing_grad = place_rows(error_grad, cell_index, total_cells).reshape(
        targets_count, n_expert, capacity, quarter
    )
    error_part = lax.all_to_all(
        outgoing_grad, "expert", split_axis=1, concat_axis=1, tiled=True
    ).reshape(targets_count, total_cells, quarter)
    segment = lax.all_gather(error_part, "layer", axis=2, tiled=True)
    block_grad = jnp.einsum("rl,trd->tld", latents, segment, preferred_element_type=jnp.float32)
    grad_lat_acc = jnp.einsum(
        "trd,tld->rl", segment, dec_weight, preferred_element_type=jnp.float32
    )
    grad_pre = (grad_lat_acc * (2.0 * active)).astype(jnp.bfloat16)
    grad_enc = jnp.einsum("rd,rl->dl", arrived, grad_pre, preferred_element_type=jnp.float32)
    grad_bias = jnp.sum(lax.optimization_barrier(grad_pre).astype(jnp.float32), axis=0)
    enc_share, dec_share, bias_share = (
        lax.psum_scatter(
            grad_enc[None].astype(jnp.bfloat16), "dp", scatter_dimension=1, tiled=True
        ).astype(jnp.float32),
        lax.psum_scatter(
            block_grad[:, None].astype(jnp.bfloat16), "dp", scatter_dimension=3, tiled=True
        ).astype(jnp.float32),
        lax.psum_scatter(
            grad_bias[None].astype(jnp.bfloat16), "dp", scatter_dimension=1, tiled=True
        ).astype(jnp.float32),
    )
    return (
        recon,
        enc_share.astype(jnp.bfloat16),
        bias_share,
        dec_share.astype(jnp.bfloat16),
        grad_b_dec,
    )


def solution(mesh):
    placed = (
        P(("expert", "dp"), None),
        P(("expert", "dp")),
        P(("expert", "dp")),
        P(("expert", "dp")),
        P("expert", None, "layer"),
        P("expert", "layer"),
        P(None, "expert", "layer", None),
        P(None, "layer"),
        P(None, ("expert", "dp"), "layer"),
    )
    return jax.shard_map(
        local,
        mesh=mesh,
        in_specs=placed,
        out_specs=(
            P(None, ("expert", "dp"), "layer"),
            P("expert", "dp", "layer"),
            P("expert", ("layer", "dp")),
            P(None, "expert", "layer", "dp"),
            P(None, "layer"),
        ),
        check_vma=False,
    )
```

profile of v0, /device:TPU:0, one launch (start us, length us, event | category | flops | bytes accessed | tf_op | source)
XLA Modules:
  0.0 428.5 jit_solution(17925462820377808188)
XLA Ops:
  7.2 0.0 copy-start
  7.2 0.0 all-reduce.3.cloned.1.call-start
  7.2 0.9 compare_select_fusion
  8.1 4.7 %scatter_custom_fusion = bf16[512,2304]{1,0:T(8,128)(2,1)} fusion(s32[256]{0:T(256)S(1)} %compare_select_fusion, bf16[256,2304]{1,0:T(8,128)(2,1)} %param.9, bf16[]{:T(256)} %constant.7.clone.1), kind=kCustom, calls=%fused_computation.24 | custom fusion | bytes 2359808 | tf_op jit(solution)/shard_map/scatter | solution.py:11
  12.8 0.0 copy-start.3
  12.8 0.0 slice-start
  12.8 60.4 %all_to_all.15 = bf16[4,128,2304]{2,1,0:T(8,128)(2,1)S(1)} all-to-all(bf16[4,128,2304]{2,1,0:T(8,128)(2,1)} %bitcast.59), channel_id=1, replica_groups=mesh['layer'=4,'expert'=4,'dp'=2] {'expert'}, dimensions={0} | all-to-all | bytes 4718592 | tf_op jit(solution)/shard_map/all_to_all | solution.py:26
  73.3 0.0 copy-start.1
  73.3 1.4 copy-done.1
  74.7 0.0 copy-done
  74.7 0.0 copy-done.3
  74.7 0.0 slice-start.1
  74.7 1.4 fusion.18
  76.1 0.0 copy-start.5
  76.1 0.9 copy-done.5
  77.0 0.0 slice-done
  77.0 0.0 slice-done.1
  77.0 4.3 %fusion = bf16[2,512,2304]{2,1,0:T(8,128)(2,1)} fusion(bf16[2,1,512,2304]{3,2,1,0:T(8,128)(2,1)S(1)} %bitcast.68, f32[512,512]{1,0:T(8,128)S(1)} %fusion.18), kind=kOutput, calls=%fused_computation.5 | convolution fusion | flops 2418802688 | bytes 10485760 | tf_op jit(solution)/shard_map/rl,tld->trd/dot_general | solution.py:33
  81.4 12.4 %copy.22 = bf16[2,512,2304]{1,0,2:T(2,128)(2,1)} copy(bf16[2,512,2304]{2,1,0:T(8,128)(2,1)} %fusion) | data formatting | bytes 9437184 | tf_op jit(solution)/shard_map/optimization_barrier | solution.py:37
  93.7 0.0 copy-start.4
  93.7 0.0 all-reduce.3.cloned.1.call-update
  93.8 0.6 copy-done.4
  94.4 0.6 dynamic-slice
  95.6 109.8 %all-reduce.3.cloned.1.call-done = bf16[2,512,2304]{1,0,2:T(2,128)(2,1)} async-done(((bf16[2,512,2304]{1,0,2:T(2,128)(2,1)}), bf16[2,512,2304]{1,0,2:T(2,128)(2,1)}) %all-reduce.3.cloned.1.call-update) | async-done | bytes 4718608
  205.4 2.1 constant_dynamic-slice_fusion
  207.5 1.6 reshape.44
  209.1 2.4 copy.23
  211.6 4.6 %all-to-all-start.1 = ((bf16[2,4,128,576]{2,3,0,1:T(8,128)(2,1)}), bf16[2,4,128,576]{2,3,0,1:T(8,128)(2,1)S(1)}, u32[]{:S(2)}, u32[]{:S(2)}) async-start(bf16[2,4,128,576]{2,3,0,1:T(8,128)(2,1)} %copy.23), calls=%async_computation.1 | async-start | bytes 2359296 | tf_op jit(solution)/shard_map/all_to_all | solution.py:43
  216.2 0.0 copy-start.2
  216.2 0.0 all-gather.2.cloned.1.call-start
  216.2 2.9 copy.25
  219.0 1.2 convert_multiply_fusion
  220.3 24.2 %all-to-all-done.1 = bf16[2,4,128,576]{2,3,0,1:T(8,128)(2,1)S(1)} async-done(((bf16[2,4,128,576]{2,3,0,1:T(8,128)(2,1)}), bf16[2,4,128,576]{2,3,0,1:T(8,128)(2,1)S(1)}, u32[]{:S(2)}, u32[]{:S(2)}) %all-to-all-start.1) | async-done | bytes 1179680 | tf_op jit(solution)/shard_map/all_to_all | solution.py:43
  244.5 3.0 copy.24
  247.5 4.2 gather_fusion
  251.7 0.0 copy-done.2
  251.7 3.3 multiply_convert_fusion
  254.9 1.7 broadcast_in_dim.8
  256.7 27.0 %scatter_fusion = bf16[2,512,576]{2,0,1:T(2,128)(2,1)} fusion(bf16[2,512,576]{2,0,1:T(2,128)(2,1)} %broadcast_in_dim.8, s32[256]{0:T(256)S(1)} %compare_select_fusion, bf16[256,2,576]{2,1,0:T(2,128)(2,1)S(1)} %bitcast.61), kind=kCustom, calls=%fused_computation.2 | custom fusion | bytes 1770496 | tf_op jit(solution)/shard_map/scatter | solution.py:11
  283.7 4.2 copy.26
  287.9 31.7 %all_to_all.16 = bf16[2,4,128,576]{2,3,0,1:T(8,128)(2,1)S(1)} all-to-all(bf16[2,4,128,576]{2,3,0,1:T(8,128)(2,1)} %copy.26), channel_id=1, replica_groups=mesh['layer'=4,'expert'=4,'dp'=2] {'expert'}, dimensions={1} | all-to-all | bytes 2359296 | tf_op jit(solution)/shard_map/all_to_all | solution.py:57
  319.5 1.1 copy_bitcast_fusion
  320.7 0.0 all-gather.2.cloned.1.call-update
  320.7 0.2 reduce-scatter.10.cloned.1.call-start
  320.9 55.0 %all-gather.2.cloned.1.call-done = bf16[2,512,2304]{1,2,0:T(8,128)(2,1)} async-done(((bf16[2,512,576]{1,2,0:T(8,128)(2,1)}), bf16[2,512,2304]{1,2,0:T(8,128)(2,1)}) %all-gather.2.cloned.1.call-update) | async-done | bytes 4718608 | tf_op jit(solution)/shard_map/all_gather | solution.py:60
  375.9 6.6 %fusion.21 = bf16[512,512]{1,0:T(8,128)(2,1)S(1)} fusion(bf16[2,512,2304]{1,2,0:T(8,128)(2,1)} %all-gather.2.cloned.1.call-done, bf16[2,1,512,2304]{3,2,1,0:T(8,128)(2,1)} %param.15, f32[512,512]{1,0:T(8,128)} %copy-done.5), kind=kOutput, calls=%fused_computation.22 | convolution fusion | flops 2416705536 | bytes 11010048 | tf_op jit(solution)/shard_map/trd,tld->rl/dot_general | solution.py:62
  382.6 0.1 reduce_sum.21
  382.7 0.8 reshape_bitcast_fusion
  383.5 0.0 reduce-scatter.10.cloned.1.call-update
  383.5 0.0 reduce-scatter.8.cloned.1.call-start
  383.5 7.4 %fusion.1 = bf16[2,1,512,2304]{2,3,0,1:T(8,128)(2,1)} fusion(bf16[2,512,2304]{1,2,0:T(8,128)(2,1)} %all-gather.2.cloned.1.call-done, f32[512,512]{1,0:T(8,128)} %copy-done.5), kind=kOutput, calls=%fused_computation.6 | convolution fusion | flops 2418802688 | bytes 10485760 | tf_op jit(solution)/shard_map/rl,trd->tld/dot_general | solution.py:61
  390.9 0.0 reduce-scatter.8.cloned.1.call-update
  390.9 0.0 reduce-scatter.6.cloned.1.call-start
  391.0 4.6 %fusion.5 = bf16[1,2304,512]{2,1,0:T(8,128)(2,1)} fusion(bf16[512,2304]{1,0:T(8,128)(2,1)} %bitcast.65, bf16[512,512]{1,0:T(8,128)(2,1)S(1)} %fusion.21), kind=kOutput, calls=%fused_computation.11 | convolution fusion | flops 1209139200 | bytes 5242880 | tf_op jit(solution)/shard_map/rd,rl->dl/dot_general | solution.py:66
  395.5 0.0 reduce-scatter.6.cloned.1.call-update
  395.6 2.9 copy.28
  398.5 0.6 convert_reduce_fusion
  399.1 17.0 %psum.7 = f32[2,576]{1,0:T(2,128)} all-reduce(f32[2,576]{1,0:T(2,128)S(1)} %convert_reduce_fusion), channel_id=1, replica_groups=mesh['layer'=4,'expert'=4,'dp'=2] {'expert','dp'}, use_global_device_ids=true, to_apply=%region_8.0 | all-reduce | flops 1152 | bytes 9216 | tf_op jit(solution)/shard_map/psum | solution.py:53
  416.1 0.0 reduce-scatter.10.cloned.1.call-done
  416.1 0.9 copy.31
  417.1 0.6 convert_element_type.79
  417.7 0.0 reduce-scatter.8.cloned.1.call-done
  417.7 4.3 %copy.29 = bf16[2,1,512,1152]{3,2,1,0:T(8,128)(2,1)} copy(bf16[2,1,512,1152]{2,3,0,1:T(8,128)(2,1)} %reduce-scatter.8.cloned.1.call-done) | data formatting | bytes 4718592
  422.0 0.0 reduce-scatter.6.cloned.1.call-done
  (2 shorter events, 0.0 us)
Async XLA Ops:
  7.2 67.5 %copy-start = (bf16[1,2304,512]{2,1,0:T(8,128)(2,1)S(1)}, bf16[1,2304,512]{2,1,0:T(8,128)(2,1)}, u32[]{:S(2)}) copy-start(bf16[1,2304,512]{2,1,0:T(8,128)(2,1)} %param.13) | copy-start | bytes 7077892
  7.2 198.3 %all-reduce.3.cloned.1.call-start = ((), (), s32[]{:S(2)}) async-start(), calls=%async_computation.10 | async-start | bytes 9437184
  12.8 61.8 %copy-start.3 = (f32[1,512]{1,0:T(1,128)S(1)}, f32[1,512]{1,0:T(1,128)}, u32[]{:S(2)}) copy-start(f32[1,512]{1,0:T(1,128)} %param.14) | copy-start | bytes 6148
  12.8 64.2 %slice-start = ((s8[4718592]{0:T(1024)(128)(4,1)}), s8[4194304]{0:T(1024)(128)(4,1)S(1)}, s32[]{:S(2)}) async-start(s8[4718592]{0:T(1024)(128)(4,1)} %bitcast.67), calls=%async_computation.11 | async-start | bytes 8388608
  73.3 1.4 copy-start.1
  74.7 2.4 slice-start.1
  76.1 1.0 copy-start.5
  93.7 0.7 copy-start.4
  211.6 33.0 %all-to-all-start.1 = ((bf16[2,4,128,576]{2,3,0,1:T(8,128)(2,1)}), bf16[2,4,128,576]{2,3,0,1:T(8,128)(2,1)S(1)}, u32[]{:S(2)}, u32[]{:S(2)}) async-start(bf16[2,4,128,576]{2,3,0,1:T(8,128)(2,1)} %copy.23), calls=%async_computation.1 | async-start | bytes 2359296 | tf_op jit(solution)/shard_map/all_to_all | solution.py:43
  216.2 35.5 %copy-start.2 = (f32[2,576]{1,0:T(2,128)S(1)}, f32[2,576]{1,0:T(2,128)}, u32[]{:S(2)}) copy-start(f32[2,576]{1,0:T(2,128)} %param.16) | copy-start | bytes 13828
  216.2 159.8 %all-gather.2.cloned.1.call-start = ((), (), s32[]{:S(2)}) async-start(), calls=%async_computation.6 | async-start | bytes 5898240 | tf_op jit(solution)/shard_map/all_gather | solution.py:60
  320.7 95.4 %reduce-scatter.10.cloned.1.call-start = ((), (), s32[]{:S(2)}) async-start(), calls=%async_computation.9 | async-start | bytes 196608
  383.5 34.2 %reduce-scatter.8.cloned.1.call-start = ((), (), s32[]{:S(2)}) async-start(), calls=%async_computation.8 | async-start | bytes 7077888 | tf_op jit(solution)/shard_map/reduce_scatter | solution.py:72
  390.9 31.0 %reduce-scatter.6.cloned.1.call-start = ((), (), s32[]{:S(2)}) async-start(), calls=%async_computation.7 | async-start | bytes 3538944 | tf_op jit(solution)/shard_map/reduce_scatter | solution.py:69
Sparse Core Ops, SparseCore 0:
  93.9 111.4 all-reduce.2
  320.8 55.0 all-gather.1
  383.6 7.5 reduce-scatter.9
  393.4 13.6 reduce-scatter.7
  409.7 11.4 reduce-scatter.5
where the time goes:
time: 430 us; the launch traced here: 429 us
  waiting for transfers between devices  189 us (44%)
  blocking collectives  109 us (25%)
  local copies, waits for them, and re-layouts  79.8 us (19%)
  matrix products  24.3 us (6%)
  between operations  14.5 us (3%)
  other arithmetic  6.69 us (2%)
  starting transfers between devices  4.94 us (1%)
    unnamed x7, waiting for transfers between devices  110 us
    all_to_all x1, blocking collectives, local(): lax.all_to_all(outgoing, 'expert', split_axis=0, concat_axis=0, tiled=True)  60.4 us
    all_gather x1, waiting for transfers between devices, local(): segment = lax.all_gather(error_part, 'layer', axis=2, tiled=True)  55 us
    scatter x2, local copies, waits for them, and re-layouts, place_rows(): return zero_fill.at[..., cell_index, :].set(values)  31.8 us
    all_to_all x1, blocking collectives, local(): lax.all_to_all(outgoing_grad, 'expert', split_axis=1, concat_axis=1, tile...  31.7 us
    all_to_all x1, waiting for transfers between devices, local(): lax.all_to_all(outgoing_rec, 'expert', split_axis=1, concat_axis=1, tiled...  24.2 us
    unnamed x23, local copies, waits for them, and re-layouts  17.5 us
    psum x1, blocking collectives, local(): grad_b_dec = lax.psum(jnp.sum(error_wide, axis=1), ('expert', 'dp'))  17 us
  transfers between devices with their start and end apart: 6, of which 3 were waited for; matrix products, arithmetic and copies ran while one was open for 6% of the time, Pallas kernels for 0%

commit v1 on v0

--- a/solution.py
+++ b/solution.py
@@ -57,7 +57,8 @@
     error_part = lax.all_to_all(
         outgoing_grad, "expert", split_axis=1, concat_axis=1, tiled=True
     ).reshape(targets_count, total_cells, quarter)
-    segment = lax.all_gather(error_part, "layer", axis=2, tiled=True)
+    blocks = lax.all_gather(error_part, "layer")
+    segment = jnp.concatenate(blocks, axis=2)
     block_grad = jnp.einsum("rl,trd->tld", latents, segment, preferred_element_type=jnp.float32)
     grad_lat_acc = jnp.einsum(
         "trd,tld->rl", segment, dec_weight, preferred_element_type=jnp.float32

time: 430 us -> 406 us (0.944)
  local copies, waits for them, and re-layouts: 79.8 us -> 58.5 us
    scatter x2, local copies, waits for them, and re-layouts: 31.8 us -> 11.9 us  [place_rows(): return zero_fill.at[..., cell_index, :].set(values)]
    unnamed x23 -> x35, local copies, waits for them, and re-layouts: 17.5 us -> 18.5 us
  transfers between devices with their start and end apart: 6 -> 6, of which waited for: 3 -> 3; matrix products, arithmetic and copies ran while one was open for 6% -> 5% of each run, Pallas kernels for 0% -> 0%
where the time goes in v1:
time: 406 us; the launch traced here: 405 us
  waiting for transfers between devices  192 us (47%)
  blocking collectives  108 us (27%)
  local copies, waits for them, and re-layouts  58.5 us (14%)
  matrix products  21.9 us (5%)
  between operations  14.6 us (4%)
  starting transfers between devices  4.9 us (1%)
  other arithmetic  4.5 us (1%)
    unnamed x7, waiting for transfers between devices  110 us
    all_to_all x1, blocking collectives, local(): lax.all_to_all(outgoing, 'expert', split_axis=0, concat_axis=0, tiled=True)  60.4 us
    all_gather x1, waiting for transfers between devices, local(): blocks = lax.all_gather(error_part, 'layer')  55.2 us
    all_to_all x1, blocking collectives, local(): lax.all_to_all(outgoing_grad, 'expert', split_axis=1, concat_axis=1, tile...  30.5 us
    all_to_all x1, waiting for transfers between devices, local(): lax.all_to_all(outgoing_rec, 'expert', split_axis=1, concat_axis=1, tiled...  27.2 us
    unnamed x35, local copies, waits for them, and re-layouts  18.5 us
    psum x1, blocking collectives, local(): grad_b_dec = lax.psum(jnp.sum(error_wide, axis=1), ('expert', 'dp'))  17 us
    optimization_barrier x1, local copies, waits for them, and re-layouts, local(): lax.optimization_barrier(partials).astype(jnp.float32).astype(jnp.bfloat16)  12.4 us
  transfers between devices with their start and end apart: 6, of which 3 were waited for; matrix products, arithmetic and copies ran while one was open for 5% of the time, Pallas kernels for 0%

profile of v1, /device:TPU:0, one launch (start us, length us, event | category | flops | bytes accessed | tf_op | source)
XLA Modules:
  0.0 404.7 jit_solution(15275040843577560385)
XLA Ops:
  7.2 0.0 copy-start
  7.2 0.0 all-reduce.3.cloned.1.call-start
  7.2 0.9 compare_select_fusion
  8.1 4.7 %scatter_custom_fusion = bf16[512,2304]{1,0:T(8,128)(2,1)} fusion(s32[256]{0:T(256)S(1)} %compare_select_fusion, bf16[256,2304]{1,0:T(8,128)(2,1)} %param.9, bf16[]{:T(256)} %constant.7.clone.1), kind=kCustom, calls=%fused_computation.23 | custom fusion | bytes 2359808 | tf_op jit(solution)/shard_map/scatter | solution.py:11
  12.8 60.4 %all_to_all.15 = bf16[4,128,2304]{2,1,0:T(8,128)(2,1)S(1)} all-to-all(bf16[4,128,2304]{2,1,0:T(8,128)(2,1)} %bitcast.59), channel_id=1, replica_groups=mesh['layer'=4,'expert'=4,'dp'=2] {'expert'}, dimensions={0} | all-to-all | bytes 4718592 | tf_op jit(solution)/shard_map/all_to_all | solution.py:26
  73.3 1.4 copy-done.4
  74.7 0.0 copy-done
  74.7 0.0 copy-done.8
  74.7 1.4 fusion.18
  76.1 0.0 copy-start.10
  76.1 0.9 copy-done.10
  77.0 0.0 slice-done
  77.0 0.0 slice-done.1
  77.0 4.3 %fusion = bf16[2,512,2304]{2,1,0:T(8,128)(2,1)} fusion(bf16[2,1,512,2304]{3,2,1,0:T(8,128)(2,1)S(1)} %bitcast.70, f32[512,512]{1,0:T(8,128)S(1)} %fusion.18), kind=kOutput, calls=%fused_computation.5 | convolution fusion | flops 2418802688 | bytes 10485760 | tf_op jit(solution)/shard_map/rl,tld->trd/dot_general | solution.py:33
  81.3 12.4 %copy.25 = bf16[2,512,2304]{1,0,2:T(2,128)(2,1)} copy(bf16[2,512,2304]{2,1,0:T(8,128)(2,1)} %fusion) | data formatting | bytes 9437184 | tf_op jit(solution)/shard_map/optimization_barrier | solution.py:37
  93.7 0.0 all-reduce.3.cloned.1.call-update
  93.8 0.6 copy-done.9
  94.4 0.6 dynamic-slice
  95.6 109.8 %all-reduce.3.cloned.1.call-done = bf16[2,512,2304]{1,0,2:T(2,128)(2,1)} async-done(((bf16[2,512,2304]{1,0,2:T(2,128)(2,1)}), bf16[2,512,2304]{1,0,2:T(2,128)(2,1)}) %all-reduce.3.cloned.1.call-update) | async-done | bytes 4718608
  205.4 2.1 constant_dynamic-slice_fusion
  207.5 0.8 reshape.47
  208.3 0.0 copy-start.5
  208.3 1.2 copy.26
  209.5 4.7 %all-to-all-start.1 = ((bf16[2,4,128,576]{2,3,0,1:T(8,128)(2,1)}), bf16[2,4,128,576]{2,3,0,1:T(8,128)(2,1)S(1)}, u32[]{:S(2)}, u32[]{:S(2)}) async-start(bf16[2,4,128,576]{2,3,0,1:T(8,128)(2,1)} %copy.26), calls=%async_computation.1 | async-start | bytes 2359296 | tf_op jit(solution)/shard_map/all_to_all | solution.py:43
  214.3 0.0 all-gather.2.cloned.1.call-start
  214.3 0.0 copy-done.5
  214.3 1.1 copy.28
  215.4 0.0 copy-done.7
  215.4 27.2 %all-to-all-done.1 = bf16[2,4,128,576]{2,3,0,1:T(8,128)(2,1)S(1)} async-done(((bf16[2,4,128,576]{2,3,0,1:T(8,128)(2,1)}), bf16[2,4,128,576]{2,3,0,1:T(8,128)(2,1)S(1)}, u32[]{:S(2)}, u32[]{:S(2)}) %all-to-all-start.1) | async-done | bytes 1179680 | tf_op jit(solution)/shard_map/all_to_all | solution.py:43
  242.6 2.9 copy.27
  245.5 3.4 gather_fusion
  248.9 0.0 copy-done.6
  248.9 2.3 multiply_convert_fusion
  251.3 0.7 broadcast_in_dim.8
  251.9 7.1 %scatter_fusion = bf16[2,512,576]{2,0,1:T(2,128)(2,1)S(1)} fusion(bf16[2,512,576]{2,0,1:T(2,128)(2,1)S(1)} %broadcast_in_dim.8, s32[256]{0:T(256)S(1)} %compare_select_fusion, bf16[256,2,576]{2,1,0:T(2,128)(2,1)S(1)} %bitcast.61), kind=kCustom, calls=%fused_computation.2 | custom fusion | bytes 1770496 | tf_op jit(solution)/shard_map/scatter | solution.py:11
  259.1 2.0 copy.29
  261.0 30.5 %all_to_all.16 = bf16[2,4,128,576]{2,3,0,1:T(8,128)(2,1)S(1)} all-to-all(bf16[2,4,128,576]{2,3,0,1:T(8,128)(2,1)S(1)} %copy.29), channel_id=1, replica_groups=mesh['layer'=4,'expert'=4,'dp'=2] {'expert'}, dimensions={1} | all-to-all | bytes 2359296 | tf_op jit(solution)/shard_map/all_to_all | solution.py:57
  291.6 0.9 copy.30
  292.5 1.3 all_gather_reshape.3
  293.8 0.0 all-gather.2.cloned.1.call-update
  293.8 0.0 copy-start.11
  293.8 0.0 reduce-scatter.10.cloned.1.call-start
  293.9 55.2 %all-gather.2.cloned.1.call-done = bf16[4,2,512,576]{2,3,1,0:T(8,128)(2,1)} async-done(((bf16[1,2,512,576]{2,3,1,0:T(8,128)(2,1)}), bf16[4,2,512,576]{2,3,1,0:T(8,128)(2,1)}) %all-gather.2.cloned.1.call-update) | async-done | bytes 4718608 | tf_op jit(solution)/shard_map/all_gather | solution.py:60
  349.0 2.6 copy.31
  351.7 0.0 copy-start.2
  351.7 2.2 copy-done.2
  353.8 0.0 copy-done.11
  353.8 5.0 %fusion.21 = bf16[512,512]{1,0:T(8,128)(2,1)S(1)} fusion(bf16[2,512,2304]{1,2,0:T(8,128)(2,1)S(1)} %bitcast.62, bf16[2,1,512,2304]{3,2,1,0:T(8,128)(2,1)} %param.15, f32[512,512]{1,0:T(8,128)S(1)} %copy-done.11), kind=kOutput, calls=%fused_computation.22 | convolution fusion | flops 2416705536 | bytes 11010048 | tf_op jit(solution)/shard_map/trd,tld->rl/dot_general | solution.py:63
  358.8 0.1 reduce_sum.21
  358.9 0.8 reshape_bitcast_fusion
  359.7 0.0 reduce-scatter.10.cloned.1.call-update
  359.8 0.0 reduce-scatter.8.cloned.1.call-start
  359.8 6.6 %fusion.1 = bf16[2,1,512,2304]{2,3,0,1:T(8,128)(2,1)} fusion(bf16[2,512,2304]{1,2,0:T(8,128)(2,1)} %bitcast.63, f32[512,512]{1,0:T(8,128)S(1)} %copy-done.11), kind=kOutput, calls=%fused_computation.6 | convolution fusion | flops 2418802688 | bytes 10485760 | tf_op jit(solution)/shard_map/rl,trd->tld/dot_general | solution.py:62
  366.4 0.0 reduce-scatter.8.cloned.1.call-update
  366.5 0.0 reduce-scatter.6.cloned.1.call-start
  366.5 4.6 %fusion.5 = bf16[1,2304,512]{2,1,0:T(8,128)(2,1)} fusion(bf16[512,2304]{1,0:T(8,128)(2,1)} %bitcast.67, bf16[512,512]{1,0:T(8,128)(2,1)S(1)} %fusion.21), kind=kOutput, calls=%fused_computation.11 | convolution fusion | flops 1209139200 | bytes 5242880 | tf_op jit(solution)/shard_map/rd,rl->dl/dot_general | solution.py:67
  371.1 0.0 reduce-scatter.6.cloned.1.call-update
  371.1 1.1 copy-done.3
  372.2 1.9 copy.33
  374.1 0.6 convert_reduce_fusion
  374.7 17.0 %psum.7 = f32[2,576]{1,0:T(2,128)} all-reduce(f32[2,576]{1,0:T(2,128)S(1)} %convert_reduce_fusion), channel_id=1, replica_groups=mesh['layer'=4,'expert'=4,'dp'=2] {'expert','dp'}, use_global_device_ids=true, to_apply=%region_8.0 | all-reduce | flops 1152 | bytes 9216 | tf_op jit(solution)/shard_map/psum | solution.py:53
  391.8 0.9 copy.37
  392.7 0.6 convert_element_type.79
  393.3 4.9 %copy.34 = bf16[2,1,512,1152]{3,2,1,0:T(8,128)(2,1)} copy(bf16[2,1,512,1152]{2,3,0,1:T(8,128)(2,1)} %reduce-scatter.8.cloned.1.call-done) | data formatting | bytes 4718592
  (16 shorter events, 0.0 us)
Async XLA Ops:
  7.2 67.5 %copy-start = (bf16[1,2304,512]{2,1,0:T(8,128)(2,1)S(1)}, bf16[1,2304,512]{2,1,0:T(8,128)(2,1)}, u32[]{:S(2)}) copy-start(bf16[1,2304,512]{2,1,0:T(8,128)(2,1)} %param.13) | copy-start | bytes 7077892
  7.2 198.2 %all-reduce.3.cloned.1.call-start = ((), (), s32[]{:S(2)}) async-start(), calls=%async_computation.10 | async-start | bytes 9437184
  12.8 61.8 %copy-start.8 = (f32[1,512]{1,0:T(1,128)S(1)}, f32[1,512]{1,0:T(1,128)}, u32[]{:S(2)}) copy-start(f32[1,512]{1,0:T(1,128)} %param.14) | copy-start | bytes 6148
  12.8 64.2 %slice-start = ((s8[4718592]{0:T(1024)(128)(4,1)}), s8[4194304]{0:T(1024)(128)(4,1)S(1)}, s32[]{:S(2)}) async-start(s8[4718592]{0:T(1024)(128)(4,1)} %bitcast.69), calls=%async_computation.11 | async-start | bytes 8388608
  73.3 1.4 copy-start.4
  74.7 2.4 slice-start.1
  76.1 1.0 copy-start.10
  93.7 0.7 copy-start.9
  208.3 6.0 %copy-start.5 = (bf16[2,256,576]{1,2,0:T(8,128)(2,1)S(1)}, bf16[2,256,576]{1,2,0:T(8,128)(2,1)}, u32[]{:S(2)}) copy-start(bf16[2,256,576]{1,2,0:T(8,128)(2,1)} %param.17) | copy-start | bytes 1769476
  209.5 5.8 %copy-start.7 = (s32[256]{0:T(256)S(1)}, s32[256]{0:T(256)}, u32[]{:S(2)}) copy-start(s32[256]{0:T(256)} %param.12) | copy-start | bytes 3076
  209.5 33.1 %all-to-all-start.1 = ((bf16[2,4,128,576]{2,3,0,1:T(8,128)(2,1)}), bf16[2,4,128,576]{2,3,0,1:T(8,128)(2,1)S(1)}, u32[]{:S(2)}, u32[]{:S(2)}) async-start(bf16[2,4,128,576]{2,3,0,1:T(8,128)(2,1)} %copy.26), calls=%async_computation.1 | async-start | bytes 2359296 | tf_op jit(solution)/shard_map/all_to_all | solution.py:43
  214.3 34.7 %copy-start.6 = (f32[2,576]{1,0:T(2,128)S(1)}, f32[2,576]{1,0:T(2,128)}, u32[]{:S(2)}) copy-start(f32[2,576]{1,0:T(2,128)} %param.16) | copy-start | bytes 13828
  214.3 134.8 %all-gather.2.cloned.1.call-start = ((), (), s32[]{:S(2)}) async-start(), calls=%async_computation.6 | async-start | bytes 5898240 | tf_op jit(solution)/shard_map/all_gather | solution.py:60
  293.8 60.0 %copy-start.11 = (f32[512,512]{1,0:T(8,128)S(1)}, f32[512,512]{1,0:T(8,128)}, u32[]{:S(2)}) copy-start(f32[512,512]{1,0:T(8,128)} %copy-done.10) | copy-start | bytes 3145732
  293.8 98.0 %reduce-scatter.10.cloned.1.call-start = ((), (), s32[]{:S(2)}) async-start(), calls=%async_computation.9 | async-start | bytes 196608
  351.7 2.2 copy-start.2
  359.8 33.5 %reduce-scatter.8.cloned.1.call-start = ((), (), s32[]{:S(2)}) async-start(), calls=%async_computation.8 | async-start | bytes 7077888 | tf_op jit(solution)/shard_map/reduce_scatter | solution.py:73
  366.5 31.7 %reduce-scatter.6.cloned.1.call-start = ((), (), s32[]{:S(2)}) async-start(), calls=%async_computation.7 | async-start | bytes 3538944 | tf_op jit(solution)/shard_map/reduce_scatter | solution.py:70
  371.1 1.1 copy-start.3
  392.7 5.5 %copy-start.1 = (bf16[1,2304,512]{2,1,0:T(8,128)(2,1)S(1)}, bf16[1,2304,512]{2,1,0:T(8,128)(2,1)}, u32[]{:S(2)}) copy-start(bf16[1,2304,512]{2,1,0:T(8,128)(2,1)} %param.13) | copy-start | bytes 7077892
Sparse Core Ops, SparseCore 0:
  93.9 111.4 all-reduce.2
  293.9 55.0 all-gather.1
  359.9 7.5 reduce-scatter.9
  369.7 13.6 reduce-scatter.7
  386.0 11.4 reduce-scatter.5
